TPU v7x, 32 devices: a whole 2x2x4 slice. The times are simulated.
32 devices in a mesh: fsdp: 4 (over z), tp: 4 (over y, core), sect: 2 (over x).
Axes of the slice: x: 2, y: 2, z: 4, core: 2. Of those that a mesh axis runs over, the one named last changes fastest.
Arguments:
- hidden: bfloat16 [4096, 8192], P('fsdp', 'sect'), may hold values from -6 to 6
- kv_weight: bfloat16 [8192, 2048], P(('sect', 'fsdp'), 'tp'), may hold values from -0.0625 to 0.0625
- readout: float32 [2048], P(('tp', 'sect')), may hold values from -0.125 to 0.125
- lengths: int32 [4, 4], P('fsdp'), may hold values from 1 to 512, as said below
- prompt_mask: int32 [4096], P('fsdp'), may hold values from 0 to 1, as said below
- group_ids: int32 [16], P('fsdp'), may hold values from 0 to 1
Outputs:
- keys_values: bfloat16 [4096, 2048], P('fsdp', ('tp', 'sect'))
- advantages: float32 [16], P('fsdp')
Inputs may be any that keep to these rules, and one draw needn't show every extreme that they name: `lengths`: each row sums to 1024; some entry of each row equals 512. `prompt_mask`: within each sequence the zeros come before the ones; at each index of fsdp exactly one sequence has no ones.
All inputs are finite; a program needn't handle non-finite values.
Results may differ from a plain program's by a relative error of at most 0.00045.
Values may be sent and summed in bfloat16 or wider, within the bound.
A program may use at most 64 MiB of HBM per device.

v0:
```python
import functools

import jax
import jax.numpy as jnp
from jax import lax
from jax.experimental import pallas as pl
from jax.experimental.pallas import tpu as pltpu
from jax.sharding import PartitionSpec as P

MESH = pl.DeviceIdType.MESH


def kernel(
    n, nt, ns, parts, tile,
    hid_any, w_any, ro_ref, mask_ref, len_ref, gid_ref,
    kv_ref, adv_ref,
    hid, wbuf, acc, precv, member, sbuf, zbuf,
    hid_sem, own_sem, wsend, wrecv, xsend, xrecv, ssend, srecv, zsend, zrecv,
):
    f, t, s = lax.axis_index("fsdp"), lax.axis_index("tp"), lax.axis_index("sect")
    plane = nt * ns
    me = t * ns + s
    rows, width = w_any.shape
    cw = width // 2
    piece = rows // parts
    by_piece = piece % 128 == 0
    tok = hid.shape[0]

    def plane_id(k):
        other = lax.rem(me + k, plane)
        return {"tp": lax.div(other, ns), "sect": lax.rem(other, ns)}

    def line_id(k):
        return {"fsdp": lax.rem(f + k, n)}

    def cols(c):
        side = s if c else 1 - s
        return pl.ds(pl.multiple_of(side * cw, cw), cw)

    def depth_at(j, r):
        return pl.ds(pl.multiple_of(j * rows + r * piece, piece), piece)

    def own_rows(c, r):
        return w_any.at[r * piece:(r + 1) * piece, cols(c)]

    def w_copy(c, j, r, step, own):
        place = wbuf.at[c, depth_at(j, r), :]
        return pltpu.make_async_remote_copy(
            src_ref=own_rows(c, r) if own else place,
            dst_ref=place,
            send_sem=wsend.at[0 if step > 0 else 1, c, r, j],
            recv_sem=wrecv.at[c, r, j],
            device_id={"fsdp": f + step},
            device_id_type=MESH,
        )

    def x_copy():
        return pltpu.make_async_remote_copy(
            src_ref=acc.at[0],
            dst_ref=precv,
            send_sem=xsend,
            recv_sem=xrecv,
            device_id={"sect": 1 - s},
            device_id_type=MESH,
        )

    def s_copy(k, slot):
        return pltpu.make_async_remote_copy(
            src_ref=sbuf.at[slot],
            dst_ref=sbuf.at[slot],
            send_sem=ssend.at[k],
            recv_sem=srecv.at[slot],
            device_id=plane_id(k),
            device_id_type=MESH,
        )

    def z_copy(k, slot):
        return pltpu.make_async_remote_copy(
            src_ref=zbuf.at[slot],
            dst_ref=zbuf.at[slot],
            send_sem=zsend.at[k],
            recv_sem=zrecv.at[slot],
            device_id=line_id(k),
            device_id_type=MESH,
        )

    def each(low, high, body):
        def step(i, carry):
            body(i)
            return carry

        lax.fori_loop(low, high, step, 0)

    barrier = pltpu.get_barrier_semaphore()
    each(1, n, lambda k: pl.semaphore_signal(
        barrier, inc=1, device_id=line_id(k), device_id_type=MESH))
    each(1, plane, lambda k: pl.semaphore_signal(
        barrier, inc=1, device_id=plane_id(k), device_id_type=MESH))

    def own_copy(c, r):
        return pltpu.make_async_copy(
            own_rows(c, r), wbuf.at[c, depth_at(f, r), :], own_sem.at[c, r])

    def send_own(c, step):
        for r in range(parts):
            w_copy(c, f, r, step, True).start()

    pl.semaphore_wait(barrier, n - 1 + plane - 1)

    @pl.when(f < n - 1)
    def _():
        send_own(0, 1)

    @pl.when(f > 0)
    def _():
        send_own(0, -1)

    @pl.when(f == 0)
    def _():
        send_own(1, 1)

    @pl.when(f == n - 1)
    def _():
        send_own(1, -1)

    hid_copy = pltpu.make_async_copy(hid_any, hid, hid_sem)
    for c in range(2):
        for r in range(parts):
            own_copy(c, r).start()
    hid_copy.start()

    place = lax.broadcasted_iota(jnp.int32, (8, tok), 1)
    seq = lax.broadcasted_iota(jnp.int32, (8, tok), 0)
    inside = jnp.zeros((8, tok), jnp.bool_)
    start = jnp.int32(0)
    n_seq = len_ref.shape[1]
    for j in range(n_seq):
        finish = start + len_ref[0, j]
        inside = inside | ((seq == j) & (place >= start) & (place < finish))
        start = finish
    member[...] = inside.astype(jnp.float32) * mask_ref[...].astype(jnp.float32)

    def add(c, depth, first):
        def product(i, carry):
            at = pl.ds(pl.multiple_of(i * tile, tile), tile)
            part = jnp.dot(
                hid[at, depth], wbuf[c, depth, :], preferred_element_type=jnp.float32)
            acc[c, at, :] = part if first else acc[c, at, :] + part
            return carry

        lax.fori_loop(0, tok // tile, product, 0)

    def arrive(c, j, r, step):
        w_copy(c, j, r, -step, False).wait_recv()

        @pl.when((f + step >= 0) & (f + step < n))
        def _():
            w_copy(c, j, r, step, False).start()

        if by_piece:
            add(c, depth_at(j, r), False)

    for c in range(2):
        for r in range(parts):
            own_copy(c, r).wait()
        if c == 0:
            hid_copy.wait()
        if by_piece:
            add(c, pl.ds(pl.multiple_of(f * rows, rows), rows), True)

        def visit(d, c=c):
            left, right = f - d, f + d
            for r in range(parts):
                @pl.when(left >= 0)
                def _():
                    arrive(c, left, r, 1)

                @pl.when(right < n)
                def _():
                    arrive(c, right, r, -1)

            if c == 0:
                @pl.when((d == f) & (f < n - 1))
                def _():
                    send_own(1, 1)

                @pl.when((d == n - 1 - f) & (f > 0))
                def _():
                    send_own(1, -1)

        each(1, n, visit)
        if not by_piece:
            add(c, slice(None), True)
        if c == 0:
            x_copy().start()

    x_copy().wait_recv()

    def finish_rows(i, carry):
        at = pl.ds(pl.multiple_of(i * tile, tile), tile)
        projected = acc[1, at, :] + precv[at, :]
        kv_ref[at, :] = projected.astype(jnp.bfloat16)
        chosen = member[:, at].astype(jnp.bfloat16)
        rest = projected
        for _ in range(3):
            digits = rest.astype(jnp.bfloat16)
            carry += jnp.dot(chosen, digits, preferred_element_type=jnp.float32)
            rest = rest - digits.astype(jnp.float32)
        return carry

    total = lax.fori_loop(
        0, tok // tile, finish_rows, jnp.zeros((8, cw), jnp.float32)) * ro_ref[...]
    sbuf[me] = total
    each(1, plane, lambda k: s_copy(k, me).start())
    count = jnp.sum(member[...], axis=1, keepdims=True)
    each(1, plane, lambda k: s_copy(k, lax.rem(me + k, plane)).wait_recv())
    seq_sum = jnp.sum(jnp.sum(sbuf[...], axis=0), axis=1, keepdims=True)
    reward = seq_sum / jnp.sqrt(jnp.maximum(count, 1.0))

    row = lax.broadcasted_iota(jnp.int32, (8, 128), 0)
    lane = lax.broadcasted_iota(jnp.int32, (8, 128), 1)
    row_gid = jnp.full((8, 128), -1, jnp.int32)
    lane_gid = jnp.full((8, 128), -2, jnp.int32)
    for j in range(n_seq):
        row_gid = jnp.where(row == j, gid_ref[j], row_gid)
        lane_gid = jnp.where(lane == j, gid_ref[j], lane_gid)
    reward = jnp.broadcast_to(reward, (8, 128))
    zbuf[f, 0] = reward
    zbuf[f, 1] = row_gid.astype(jnp.float32)
    each(1, n, lambda k: z_copy(k, f).start())
    mine = jnp.sum(jnp.where(row == lane, reward, 0.0), axis=0, keepdims=True)
    each(1, n, lambda k: z_copy(k, lax.rem(f + k, n)).wait_recv())
    same = (zbuf[:, 1] == lane_gid.astype(jnp.float32)[None]).astype(jnp.float32)
    rewards = zbuf[:, 0]

    def over(value):
        return jnp.sum(jnp.sum(value, axis=0), axis=0, keepdims=True)

    size = jnp.maximum(over(same), 1.0)
    mean = over(same * rewards) / size
    var = over(same * (rewards - mean[None]) ** 2) / size
    adv_ref[...] = ((mine - mean) / jnp.sqrt(var + 1.0))[:, :n_seq]

    each(1, plane, lambda k: s_copy(k, me).wait_send())
    each(1, n, lambda k: z_copy(k, f).wait_send())
    x_copy().wait_send()
    for c in range(2):
        def sent(j, c=c):
            for r in range(parts):
                @pl.when((j <= f) & (f < n - 1))
                def _():
                    w_copy(c, j, r, 1, False).wait_send()

                @pl.when((j >= f) & (f > 0))
                def _():
                    w_copy(c, j, r, -1, False).wait_send()

        each(0, n, sent)


def solution(mesh):
    n, nt, ns = mesh.shape["fsdp"], mesh.shape["tp"], mesh.shape["sect"]

    def local(hidden, kv_weight, readout, lengths, prompt_mask, group_ids):
        tok, depth = hidden.shape
        rows, width = kv_weight.shape
        parts = max(1, min(2, rows // 256))
        cw = width // 2
        plane = nt * ns
        n_seq = lengths.shape[1]
        dma = pltpu.SemaphoreType.DMA
        vmem, smem, anywhere = (
            pl.BlockSpec(memory_space=pltpu.VMEM),
            pl.BlockSpec(memory_space=pltpu.SMEM),
            pl.BlockSpec(memory_space=pl.ANY),
        )
        kv, adv = pl.pallas_call(
            functools.partial(kernel, n, nt, ns, parts, min(256, tok)),
            out_shape=(
                pltpu.VMEM((tok, width // 2), jnp.bfloat16),
                pltpu.VMEM((1, n_seq), jnp.float32),
            ),
            in_specs=[anywhere, anywhere, vmem, vmem, smem, smem],
            out_specs=(vmem, vmem),
            scratch_shapes=[
                pltpu.VMEM((tok, depth), jnp.bfloat16),
                pltpu.VMEM((2, depth, cw), jnp.bfloat16),
                pltpu.VMEM((2, tok, cw), jnp.float32),
                pltpu.VMEM((tok, cw), jnp.float32),
                pltpu.VMEM((8, tok), jnp.float32),
                pltpu.VMEM((plane, 8, cw), jnp.float32),
                pltpu.VMEM((n, 2, 8, 128), jnp.float32),
                dma, dma((2, parts)),
                dma((2, 2, parts, n)), dma((2, parts, n)),
                dma, dma,
                dma((plane,)), dma((plane,)),
                dma((n,)), dma((n,)),
            ],
            compiler_params=pltpu.CompilerParams(collective_id=0, has_side_effects=True),
        )(hidden, kv_weight, readout[None, :], prompt_mask[None, :], lengths, group_ids)
        return kv, adv[0]

    return jax.shard_map(
        local,
        mesh=mesh,
        in_specs=(
            P("fsdp", "sect"),
            P(("sect", "fsdp"), "tp"),
            P(("tp", "sect")),
            P("fsdp", None),
            P("fsdp"),
            P("fsdp"),
        ),
        out_specs=(P("fsdp", ("tp", "sect")), P("fsdp")),
        check_vma=False,
    )
```

profile of v0, /device:TPU:0, one launch (start us, length us, event | category | flops | bytes accessed | tf_op | source)
XLA Modules:
  0.0 86.7 jit_solution(10991666208309042142)
XLA Ops:
  0.6 84.8 %shard_map.77 = (bf16[1024,256]{1,0:T(8,128)(2,1)S(1)}, f32[1,4]{1,0:T(1,128)S(1)}) custom-call(bf16[1024,4096]{1,0:T(8,128)(2,1)} %hid_any.1, bf16[1024,512]{1,0:T(8,128)(2,1)} %w_any.1, f32[1,256]{1,0:T(1,128)} %bitcast.5, s32[1,1024]{1,0:T(1,128)} %bitcast.4, s32[1,4]{1,0:T(1,128)} %len_ref.1, s32[4]{0:T(128)} %gid_ref.1), custom_call_target="tpu_custom_call" | custom-call | tf_op jit(solution)/shard_map/pallas_call | solution.py:277
  85.4 0.8 copy.10
  86.2 0.5 copy.11
where the time goes:
time: 86.9 us; the launch traced here: 86.7 us
  Pallas kernels  84.8 us (98%)
  local copies, waits for them, and re-layouts  1.31 us (2%)
    pallas_call x1, Pallas kernels, local(): pl.pallas_call(functools.partial(kernel, n, nt, ns, parts, min(256, tok))...  84.8 us

commit v1 on v0

--- a/solution.py
+++ b/solution.py
@@ -258,6 +258,304 @@
         each(0, n, sent)
 
 
+def line_kernel(
+    nt, ns, parts, tile,
+    hid_any, w_any, ro_ref, mask_ref, len_ref, gid_ref,
+    kv_ref, adv_ref,
+    hid, wbuf, acc, precv, member, gsum, robuf, vbuf, sbuf, zbuf,
+    hid_sem, own_sem, wsend, wrecv, xsend, xrecv, rsend, rrecv,
+    vsend, vrecv, ssend, srecv, zsend, zrecv,
+):
+    n = 4
+    f, t, s = lax.axis_index("fsdp"), lax.axis_index("tp"), lax.axis_index("sect")
+    plane = nt * ns
+    me = t * ns + s
+    rows, width = w_any.shape
+    cw = width // 2
+    piece = rows // parts
+    tok, depth = hid.shape
+    tiles = tok // tile
+    inward = jnp.where(f < 2, 1, -1)
+    outer = (f == 0) | (f == n - 1)
+    inner = (f == 1) | (f == n - 2)
+
+    def plane_id(k):
+        other = lax.rem(me + k, plane)
+        return {"tp": lax.div(other, ns), "sect": lax.rem(other, ns)}
+
+    def line_id(k):
+        return {"fsdp": lax.rem(f + k, n)}
+
+    def cols(c):
+        side = s if c else 1 - s
+        return pl.ds(pl.multiple_of(side * cw, cw), cw)
+
+    def depth_at(j, r):
+        return pl.ds(pl.multiple_of(j * rows + r * piece, piece), piece)
+
+    def block_at(j):
+        return pl.ds(pl.multiple_of(j * rows, rows), rows)
+
+    def remote(src, dst, send, recv, device):
+        return pltpu.make_async_remote_copy(
+            src_ref=src, dst_ref=dst, send_sem=send, recv_sem=recv,
+            device_id=device, device_id_type=MESH)
+
+    def w_copy(c, j, r, step, own=False):
+        place = wbuf.at[c, depth_at(j, r), :]
+        src = w_any.at[r * piece:(r + 1) * piece, cols(c)] if own else place
+        toward = 0 if step is inward else 1
+        return remote(src, place, wsend.at[toward, c, r, j], wrecv.at[c, r, j], {"fsdp": f + step})
+
+    def x_copy(i):
+        at = pl.ds(pl.multiple_of(i * tile, tile), tile)
+        return remote(acc.at[0, at], precv.at[at], xsend.at[i], xrecv.at[i], {"sect": 1 - s})
+
+    def r_copy():
+        return remote(ro_ref, robuf, rsend, rrecv, {"sect": 1 - s})
+
+    def v_copy(k, slot):
+        return remote(vbuf.at[slot], vbuf.at[slot], vsend.at[k], vrecv.at[slot], line_id(k))
+
+    def s_copy(k, slot):
+        return remote(sbuf.at[slot], sbuf.at[slot], ssend.at[k], srecv.at[slot], plane_id(k))
+
+    def z_copy(k, slot):
+        return remote(zbuf.at[slot], zbuf.at[slot], zsend.at[k], zrecv.at[slot], line_id(k))
+
+    def own_copy(c):
+        return pltpu.make_async_copy(
+            w_any.at[:, cols(c)], wbuf.at[c, block_at(f), :], own_sem.at[c])
+
+    def each(low, high, body):
+        def step(i, carry):
+            body(i)
+            return carry
+
+        lax.fori_loop(low, high, step, 0)
+
+    outward = -inward
+
+    def send_own(c, r, step):
+        w_copy(c, f, r, step, own=True).start()
+
+    def take(c, j, r, step=None):
+        w_copy(c, j, r, outward).wait_recv()
+        if step is not None:
+            w_copy(c, j, r, step).start()
+
+    barrier = pltpu.get_barrier_semaphore()
+    each(1, n, lambda k: pl.semaphore_signal(
+        barrier, inc=1, device_id=line_id(k), device_id_type=MESH))
+    each(1, plane, lambda k: pl.semaphore_signal(
+        barrier, inc=1, device_id=plane_id(k), device_id_type=MESH))
+    hid_copy = pltpu.make_async_copy(hid_any, hid, hid_sem)
+    for c in (1, 0):
+        own_copy(c).start()
+    hid_copy.start()
+    pl.semaphore_wait(barrier, n - 1 + plane - 1)
+
+    for r in range(parts):
+        send_own(0, r, inward)
+
+        @pl.when(inner)
+        def _():
+            send_own(0, r, outward)
+    r_copy().start()
+
+    place = lax.broadcasted_iota(jnp.int32, (8, tok), 1)
+    seq = lax.broadcasted_iota(jnp.int32, (8, tok), 0)
+    inside = jnp.zeros((8, tok), jnp.bool_)
+    start = jnp.int32(0)
+    n_seq = len_ref.shape[1]
+    for j in range(n_seq):
+        finish = start + len_ref[0, j]
+        inside = inside | ((seq == j) & (place >= start) & (place < finish))
+        start = finish
+    member[...] = inside.astype(jnp.float32) * mask_ref[...].astype(jnp.float32)
+
+    def weigh():
+        line = lax.broadcasted_iota(jnp.int32, (8, cw), 0)
+        total = jnp.zeros((8, rows), jnp.float32)
+        for c in (1, 0):
+            if c == 0:
+                r_copy().wait_recv()
+            own_copy(c).wait()
+            rest = jnp.broadcast_to((ro_ref if c else robuf)[...], (8, cw))
+            digits = jnp.zeros((8, cw), jnp.float32)
+            for k in range(3):
+                digit = rest.astype(jnp.bfloat16).astype(jnp.float32)
+                digits = jnp.where(line == k, digit, digits)
+                rest = rest - digit
+            total += lax.dot_general(
+                digits.astype(jnp.bfloat16), wbuf[c, block_at(f), :],
+                (((1,), (1,)), ((), ())), preferred_element_type=jnp.float32)
+        total = jnp.sum(total, axis=0, keepdims=True)
+        for i in range(rows // 128):
+            vbuf[f, i:i + 1, :] = total[:, i * 128:(i + 1) * 128]
+        for k in range(1, n):
+            v_copy(k, f).start()
+
+    def gather_tokens():
+        hid_copy.wait()
+        chosen = member[...].astype(jnp.bfloat16)
+        step = 512 if depth % 512 == 0 else 128
+
+        def part(i):
+            at = pl.ds(pl.multiple_of(i * step, step), step)
+            gsum[:, at] = jnp.dot(chosen, hid[:, at], preferred_element_type=jnp.float32)
+
+        each(0, depth // step, part)
+
+    def score():
+        for k in range(1, n):
+            v_copy(k, lax.rem(f + k, n)).wait_recv()
+        total = jnp.zeros((8, 128), jnp.float32)
+        for j in range(n):
+            for i in range(rows // 128):
+                at = j * rows + i * 128
+                total += gsum[:, at:at + 128] * vbuf[j, i:i + 1, :]
+        sbuf[me] = jnp.broadcast_to(jnp.sum(total, axis=1, keepdims=True), (8, 128))
+        each(1, plane, lambda k: s_copy(k, me).start())
+
+    row = lax.broadcasted_iota(jnp.int32, (8, 128), 0)
+    lane = lax.broadcasted_iota(jnp.int32, (8, 128), 1)
+
+    def reward():
+        count = jnp.sum(member[...], axis=1, keepdims=True)
+        each(1, plane, lambda k: s_copy(k, lax.rem(me + k, plane)).wait_recv())
+        seq_sum = jnp.sum(sbuf[...], axis=0)
+        row_gid = jnp.full((8, 128), -1, jnp.int32)
+        for j in range(n_seq):
+            row_gid = jnp.where(row == j, gid_ref[j], row_gid)
+        zbuf[f, 0] = seq_sum / jnp.sqrt(jnp.maximum(count, 1.0))
+        zbuf[f, 1] = row_gid.astype(jnp.float32)
+        each(1, n, lambda k: z_copy(k, f).start())
+
+    def advantage():
+        each(1, n, lambda k: z_copy(k, lax.rem(f + k, n)).wait_recv())
+        lane_gid = jnp.full((8, 128), -2, jnp.int32)
+        for j in range(n_seq):
+            lane_gid = jnp.where(lane == j, gid_ref[j], lane_gid)
+        mine = jnp.sum(jnp.where(row == lane, zbuf[f, 0], 0.0), axis=0, keepdims=True)
+        same = (zbuf[:, 1] == lane_gid.astype(jnp.float32)[None]).astype(jnp.float32)
+        rewards = zbuf[:, 0]
+
+        def over(value):
+            return jnp.sum(jnp.sum(value, axis=0), axis=0, keepdims=True)
+
+        size = jnp.maximum(over(same), 1.0)
+        mean = over(same * rewards) / size
+        var = over(same * (rewards - mean[None]) ** 2) / size
+        adv_ref[...] = ((mine - mean) / jnp.sqrt(var + 1.0))[:, :n_seq]
+
+    def add(c, at_depth, first=False, send=False):
+        def product(i):
+            at = pl.ds(pl.multiple_of(i * tile, tile), tile)
+            part = jnp.dot(
+                hid[at, at_depth], wbuf[c, at_depth, :], preferred_element_type=jnp.float32)
+            acc[c, at, :] = part if first else acc[c, at, :] + part
+            if send:
+                x_copy(i).start()
+
+        each(0, tiles, product)
+
+    def finish(at_depth):
+        def product(i):
+            at = pl.ds(pl.multiple_of(i * tile, tile), tile)
+            part = jnp.dot(
+                hid[at, at_depth], wbuf[1, at_depth, :], preferred_element_type=jnp.float32)
+            kv_ref[at, :] = (acc[1, at, :] + precv[at, :] + part).astype(jnp.bfloat16)
+
+        each(0, tiles, product)
+
+    weigh()
+
+    @pl.when(outer)
+    def _():
+        mid, far, end = f + inward, f + 2 * inward, f + 3 * inward
+        for r in range(parts):
+            send_own(1, r, inward)
+        gather_tokens()
+        for c in range(2):
+            add(c, block_at(f), first=True)
+        for r in range(parts):
+            take(0, mid, r)
+        add(0, block_at(mid))
+        score()
+        for r in range(parts):
+            take(0, far, r)
+        add(0, block_at(far))
+        reward()
+        for r in range(parts):
+            take(0, end, r)
+        add(0, block_at(end), send=True)
+        for r in range(parts):
+            take(1, mid, r)
+        add(1, block_at(mid))
+        advantage()
+        for r in range(parts):
+            take(1, far, r)
+        add(1, block_at(far))
+        for r in range(parts - 1):
+            take(1, end, r)
+            add(1, depth_at(end, r))
+        each(0, tiles, lambda i: x_copy(i).wait_recv())
+        take(1, end, parts - 1)
+        finish(depth_at(end, parts - 1))
+
+    @pl.when(inner)
+    def _():
+        mine, edge, far, end = f, f + outward, f + inward, f + 2 * inward
+        send_own(1, 0, outward)
+        for r in range(parts):
+            take(0, edge, r, inward)
+        for r in range(parts):
+            send_own(1, r, inward)
+        for r in range(parts):
+            take(0, far, r, outward)
+        gather_tokens()
+        add(0, block_at(mine), first=True)
+        for r in range(parts):
+            take(0, end, r, outward)
+        for r in range(1, parts):
+            send_own(1, r, outward)
+        score()
+        for r in range(parts):
+            take(1, edge, r, inward)
+        add(0, block_at(edge))
+        add(0, block_at(far))
+        reward()
+        add(0, block_at(end), send=True)
+        for r in range(parts):
+            take(1, far, r, outward)
+        add(1, block_at(mine), first=True)
+        add(1, block_at(edge))
+        for r in range(parts):
+            take(1, end, r, outward)
+        add(1, block_at(far))
+        advantage()
+        each(0, tiles, lambda i: x_copy(i).wait_recv())
+        finish(block_at(end))
+
+    each(0, tiles, lambda i: x_copy(i).wait_send())
+    r_copy().wait_send()
+    for k in range(1, n):
+        v_copy(k, f).wait_send()
+    each(1, plane, lambda k: s_copy(k, me).wait_send())
+    each(1, n, lambda k: z_copy(k, f).wait_send())
+    for c in range(2):
+        for r in range(parts):
+            w_copy(c, f, r, inward).wait_send()
+
+            @pl.when(inner)
+            def _():
+                w_copy(c, f, r, outward).wait_send()
+                w_copy(c, f + outward, r, inward).wait_send()
+                w_copy(c, f + inward, r, outward).wait_send()
+                w_copy(c, f + 2 * inward, r, outward).wait_send()
+
+
 def solution(mesh):
     n, nt, ns = mesh.shape["fsdp"], mesh.shape["tp"], mesh.shape["sect"]
 
@@ -268,21 +566,39 @@
         cw = width // 2
         plane = nt * ns
         n_seq = lengths.shape[1]
+        tile = min(256, tok)
+        in_line = n == 4 and ns == 2 and rows % 1024 == 0 and cw % 128 == 0 and tok % tile == 0
         dma = pltpu.SemaphoreType.DMA
         vmem, smem, anywhere = (
             pl.BlockSpec(memory_space=pltpu.VMEM),
             pl.BlockSpec(memory_space=pltpu.SMEM),
             pl.BlockSpec(memory_space=pl.ANY),
         )
-        kv, adv = pl.pallas_call(
-            functools.partial(kernel, n, nt, ns, parts, min(256, tok)),
-            out_shape=(
-                pltpu.VMEM((tok, width // 2), jnp.bfloat16),
-                pltpu.VMEM((1, n_seq), jnp.float32),
-            ),
-            in_specs=[anywhere, anywhere, vmem, vmem, smem, smem],
-            out_specs=(vmem, vmem),
-            scratch_shapes=[
+        if in_line:
+            body = functools.partial(line_kernel, nt, ns, parts, tile)
+            tiles = tok // tile
+            scratch = [
+                pltpu.VMEM((tok, depth), jnp.bfloat16),
+                pltpu.VMEM((2, depth, cw), jnp.bfloat16),
+                pltpu.VMEM((2, tok, cw), jnp.float32),
+                pltpu.VMEM((tok, cw), jnp.float32),
+                pltpu.VMEM((8, tok), jnp.float32),
+                pltpu.VMEM((8, depth), jnp.float32),
+                pltpu.VMEM((1, cw), jnp.float32),
+                pltpu.VMEM((n, rows // 128, 128), jnp.float32),
+                pltpu.VMEM((plane, 8, 128), jnp.float32),
+                pltpu.VMEM((n, 2, 8, 128), jnp.float32),
+                dma, dma((2,)),
+                dma((2, 2, parts, n)), dma((2, parts, n)),
+                dma((tiles,)), dma((tiles,)),
+                dma, dma,
+                dma((n,)), dma((n,)),
+                dma((plane,)), dma((plane,)),
+                dma((n,)), dma((n,)),
+            ]
+        else:
+            body = functools.partial(kernel, n, nt, ns, parts, tile)
+            scratch = [
                 pltpu.VMEM((tok, depth), jnp.bfloat16),
                 pltpu.VMEM((2, depth, cw), jnp.bfloat16),
                 pltpu.VMEM((2, tok, cw), jnp.float32),
@@ -295,7 +611,16 @@
                 dma, dma,
                 dma((plane,)), dma((plane,)),
                 dma((n,)), dma((n,)),
-            ],
+            ]
+        kv, adv = pl.pallas_call(
+            body,
+            out_shape=(
+                pltpu.VMEM((tok, width // 2), jnp.bfloat16),
+                pltpu.VMEM((1, n_seq), jnp.float32),
+            ),
+            in_specs=[anywhere, anywhere, vmem, vmem, smem, smem],
+            out_specs=(vmem, vmem),
+            scratch_shapes=scratch,
             compiler_params=pltpu.CompilerParams(collective_id=0, has_side_effects=True),
         )(hidden, kv_weight, readout[None, :], prompt_mask[None, :], lengths, group_ids)
         return kv, adv[0]

time: 86.9 us -> 79.9 us (0.919)
  Pallas kernels: 84.8 us -> 77.8 us
    pallas_call x1, Pallas kernels: 84.8 us -> 77.8 us  [local(): pl.pallas_call(body, out_shape=(pltpu.VMEM((tok, width // 2), jnp.bfloat1...]
where the time goes in v1:
time: 79.9 us; the launch traced here: 79.7 us
  Pallas kernels  77.8 us (97%)
  local copies, waits for them, and re-layouts  1.31 us (2%)
    pallas_call x1, Pallas kernels, local(): pl.pallas_call(body, out_shape=(pltpu.VMEM((tok, width // 2), jnp.bfloat1...  77.8 us

profile of v1, /device:TPU:0, one launch (start us, length us, event | category | flops | bytes accessed | tf_op | source)
XLA Modules:
  0.0 79.7 jit_solution(9834777458662791853)
XLA Ops:
  0.6 77.8 %shard_map.77 = (bf16[1024,256]{1,0:T(8,128)(2,1)S(1)}, f32[1,4]{1,0:T(1,128)S(1)}) custom-call(bf16[1024,4096]{1,0:T(8,128)(2,1)} %hid_any.1, bf16[1024,512]{1,0:T(8,128)(2,1)} %w_any.1, f32[1,256]{1,0:T(1,128)} %bitcast.5, s32[1,1024]{1,0:T(1,128)} %bitcast.4, s32[1,4]{1,0:T(1,128)} %len_ref.1, s32[4]{0:T(128)} %gid_ref.1), custom_call_target="tpu_custom_call" | custom-call | tf_op jit(solution)/shard_map/pallas_call | solution.py:615
  78.4 0.8 copy.10
  79.2 0.5 copy.11

commit v2 on v1

--- a/solution.py
+++ b/solution.py
@@ -262,9 +262,10 @@
     nt, ns, parts, tile,
     hid_any, w_any, ro_ref, mask_ref, len_ref, gid_ref,
     kv_ref, adv_ref,
-    hid, wbuf, acc, precv, member, gsum, robuf, vbuf, sbuf, zbuf,
+    hid, wbuf, acc, precv, hbuf, racc, rx, rret, member, gsum, robuf, vbuf, sbuf, zbuf,
     hid_sem, own_sem, wsend, wrecv, xsend, xrecv, rsend, rrecv,
     vsend, vrecv, ssend, srecv, zsend, zrecv,
+    hsend, hrecv, qsend, qrecv, bsend, brecv,
 ):
     n = 4
     f, t, s = lax.axis_index("fsdp"), lax.axis_index("tp"), lax.axis_index("sect")
@@ -272,12 +273,21 @@
     me = t * ns + s
     rows, width = w_any.shape
     cw = width // 2
+    qw = cw // 2
     piece = rows // parts
     tok, depth = hid.shape
     tiles = tok // tile
+    share = tile // nt
     inward = jnp.where(f < 2, 1, -1)
+    outward = -inward
     outer = (f == 0) | (f == n - 1)
     inner = (f == 1) | (f == n - 2)
+    near_at = jnp.where(f < 2, 0, 2 * rows)
+    near = pl.ds(pl.multiple_of(near_at, rows), 2 * rows)
+    far = pl.ds(pl.multiple_of(2 * rows - near_at, rows), 2 * rows)
+    mate = lax.div(t, 2) * 2 + (1 - lax.rem(t, 2))
+    across = lax.rem(t + 2, 4)
+    cross = lax.rem(mate + 2, 4)
 
     def plane_id(k):
         other = lax.rem(me + k, plane)
@@ -286,30 +296,58 @@
     def line_id(k):
         return {"fsdp": lax.rem(f + k, n)}
 
-    def cols(c):
-        side = s if c else 1 - s
-        return pl.ds(pl.multiple_of(side * cw, cw), cw)
+    def cols(q):
+        side = s if q >= 2 else 1 - s
+        return pl.ds(pl.multiple_of(side * cw + (q % 2) * qw, qw), qw)
 
     def depth_at(j, r):
         return pl.ds(pl.multiple_of(j * rows + r * piece, piece), piece)
 
     def block_at(j):
         return pl.ds(pl.multiple_of(j * rows, rows), rows)
+
+    def tile_at(i):
+        return pl.ds(pl.multiple_of(i * tile, tile), tile)
+
+    def share_at(i, p):
+        return pl.ds(pl.multiple_of(i * tile + p * share, share), share)
 
     def remote(src, dst, send, recv, device):
         return pltpu.make_async_remote_copy(
             src_ref=src, dst_ref=dst, send_sem=send, recv_sem=recv,
             device_id=device, device_id_type=MESH)
 
-    def w_copy(c, j, r, step, own=False):
-        place = wbuf.at[c, depth_at(j, r), :]
-        src = w_any.at[r * piece:(r + 1) * piece, cols(c)] if own else place
+    def w_copy(q, j, r, step, own=False):
+        place = wbuf.at[q, depth_at(j, r), :]
+        src = w_any.at[r * piece:(r + 1) * piece, cols(q)] if own else place
         toward = 0 if step is inward else 1
-        return remote(src, place, wsend.at[toward, c, r, j], wrecv.at[c, r, j], {"fsdp": f + step})
-
-    def x_copy(i):
-        at = pl.ds(pl.multiple_of(i * tile, tile), tile)
-        return remote(acc.at[0, at], precv.at[at], xsend.at[i], xrecv.at[i], {"sect": 1 - s})
+        return remote(src, place, wsend.at[toward, q, r, j], wrecv.at[q, r, j], {"fsdp": f + step})
+
+    def x_copy(q, i):
+        at = tile_at(i)
+        return remote(acc.at[q, at], precv.at[q, at], xsend.at[q, i], xrecv.at[q, i], {"sect": 1 - s})
+
+    def h_copy(i):
+        at = share_at(i, t)
+        return remote(hid.at[at, far], hbuf.at[at], hsend.at[0, i], hrecv.at[i, t], {"fsdp": f + inward})
+
+    def h_spread(k, i):
+        p = (t, t, across)[k]
+        to = (mate, across, mate)[k]
+        at = share_at(i, p)
+        return remote(hbuf.at[at], hbuf.at[at], hsend.at[k, i], hrecv.at[i, p], {"tp": to})
+
+    def h_recv(i, p):
+        at = share_at(i, p)
+        return remote(hbuf.at[at], hbuf.at[at], hsend.at[0, i], hrecv.at[i, p], {"tp": mate})
+
+    def q_copy(i):
+        at = tile_at(i)
+        return remote(racc.at[0, at], rx.at[at], qsend.at[i], qrecv.at[i], {"sect": 1 - s})
+
+    def b_copy(i):
+        at = tile_at(i)
+        return remote(racc.at[1, at], rret.at[at], bsend.at[i], brecv.at[i], {"fsdp": f + outward})
 
     def r_copy():
         return remote(ro_ref, robuf, rsend, rrecv, {"sect": 1 - s})
@@ -323,9 +361,9 @@
     def z_copy(k, slot):
         return remote(zbuf.at[slot], zbuf.at[slot], zsend.at[k], zrecv.at[slot], line_id(k))
 
-    def own_copy(c):
+    def own_copy(q):
         return pltpu.make_async_copy(
-            w_any.at[:, cols(c)], wbuf.at[c, block_at(f), :], own_sem.at[c])
+            w_any.at[:, cols(q)], wbuf.at[q, block_at(f), :], own_sem.at[q])
 
     def each(low, high, body):
         def step(i, carry):
@@ -334,33 +372,33 @@
 
         lax.fori_loop(low, high, step, 0)
 
-    outward = -inward
-
-    def send_own(c, r, step):
-        w_copy(c, f, r, step, own=True).start()
-
-    def take(c, j, r, step=None):
-        w_copy(c, j, r, outward).wait_recv()
-        if step is not None:
-            w_copy(c, j, r, step).start()
+    def send_own(q, step):
+        for r in range(parts):
+            w_copy(q, f, r, step, own=True).start()
+
+    def take(q, j, step=None):
+        for r in range(parts):
+            w_copy(q, j, r, outward).wait_recv()
+            if step is not None:
+                w_copy(q, j, r, step).start()
 
     barrier = pltpu.get_barrier_semaphore()
     each(1, n, lambda k: pl.semaphore_signal(
         barrier, inc=1, device_id=line_id(k), device_id_type=MESH))
     each(1, plane, lambda k: pl.semaphore_signal(
         barrier, inc=1, device_id=plane_id(k), device_id_type=MESH))
+    for q in (2, 3, 0, 1):
+        own_copy(q).start()
     hid_copy = pltpu.make_async_copy(hid_any, hid, hid_sem)
-    for c in (1, 0):
-        own_copy(c).start()
     hid_copy.start()
     pl.semaphore_wait(barrier, n - 1 + plane - 1)
 
-    for r in range(parts):
-        send_own(0, r, inward)
-
-        @pl.when(inner)
-        def _():
-            send_own(0, r, outward)
+    send_own(0, inward)
+
+    @pl.when(inner)
+    def _():
+        send_own(0, outward)
+
     r_copy().start()
 
     place = lax.broadcasted_iota(jnp.int32, (8, tok), 1)
@@ -375,20 +413,21 @@
     member[...] = inside.astype(jnp.float32) * mask_ref[...].astype(jnp.float32)
 
     def weigh():
-        line = lax.broadcasted_iota(jnp.int32, (8, cw), 0)
+        line = lax.broadcasted_iota(jnp.int32, (8, qw), 0)
         total = jnp.zeros((8, rows), jnp.float32)
-        for c in (1, 0):
-            if c == 0:
+        for q in (2, 3, 0, 1):
+            if q == 0:
                 r_copy().wait_recv()
-            own_copy(c).wait()
-            rest = jnp.broadcast_to((ro_ref if c else robuf)[...], (8, cw))
-            digits = jnp.zeros((8, cw), jnp.float32)
+            own_copy(q).wait()
+            values = (ro_ref if q >= 2 else robuf)[:, (q % 2) * qw:(q % 2 + 1) * qw]
+            rest = jnp.broadcast_to(values, (8, qw))
+            digits = jnp.zeros((8, qw), jnp.float32)
             for k in range(3):
                 digit = rest.astype(jnp.bfloat16).astype(jnp.float32)
                 digits = jnp.where(line == k, digit, digits)
                 rest = rest - digit
             total += lax.dot_general(
-                digits.astype(jnp.bfloat16), wbuf[c, block_at(f), :],
+                digits.astype(jnp.bfloat16), wbuf[q, block_at(f), :],
                 (((1,), (1,)), ((), ())), preferred_element_type=jnp.float32)
         total = jnp.sum(total, axis=0, keepdims=True)
         for i in range(rows // 128):
@@ -397,7 +436,6 @@
             v_copy(k, f).start()
 
     def gather_tokens():
-        hid_copy.wait()
         chosen = member[...].astype(jnp.bfloat16)
         step = 512 if depth % 512 == 0 else 128
 
@@ -449,111 +487,172 @@
         var = over(same * (rewards - mean[None]) ** 2) / size
         adv_ref[...] = ((mine - mean) / jnp.sqrt(var + 1.0))[:, :n_seq]
 
-    def add(c, at_depth, first=False, send=False):
+    def add(q, at_depth, first=False, send=False, low=0, high=tiles):
         def product(i):
-            at = pl.ds(pl.multiple_of(i * tile, tile), tile)
+            at = tile_at(i)
             part = jnp.dot(
-                hid[at, at_depth], wbuf[c, at_depth, :], preferred_element_type=jnp.float32)
-            acc[c, at, :] = part if first else acc[c, at, :] + part
+                hid[at, at_depth], wbuf[q, at_depth, :], preferred_element_type=jnp.float32)
+            acc[q, at, :] = part if first else acc[q, at, :] + part
             if send:
-                x_copy(i).start()
+                x_copy(q, i).start()
+
+        each(low, high, product)
+
+    whole = slice(None)
+
+    def out_at(q):
+        return slice((q - 2) * qw, (q - 1) * qw)
+
+    def finish(q, at_depth):
+        def product(i):
+            at = tile_at(i)
+            x_copy(q - 2, i).wait_recv()
+            part = jnp.dot(
+                hid[at, at_depth], wbuf[q, at_depth, :], preferred_element_type=jnp.float32)
+            kv_ref[at, out_at(q)] = (acc[q, at, :] + precv[q - 2, at, :] + part).astype(jnp.bfloat16)
 
         each(0, tiles, product)
 
-    def finish(at_depth):
-        def product(i):
-            at = pl.ds(pl.multiple_of(i * tile, tile), tile)
-            part = jnp.dot(
-                hid[at, at_depth], wbuf[1, at_depth, :], preferred_element_type=jnp.float32)
-            kv_ref[at, :] = (acc[1, at, :] + precv[at, :] + part).astype(jnp.bfloat16)
-
-        each(0, tiles, product)
+    def spread(i):
+        h_recv(i, t).wait_recv()
+        h_spread(0, i).start()
+        h_spread(1, i).start()
+
+    def partial(i):
+        h_recv(i, across).wait_recv()
+        h_spread(2, i).start()
+        h_recv(i, mate).wait_recv()
+        h_recv(i, cross).wait_recv()
+        at = tile_at(i)
+        racc[0, at, :] = jnp.dot(hbuf[at, :], wbuf[0, far, :], preferred_element_type=jnp.float32)
+        q_copy(i).start()
+
+    def give_back(i):
+        at = tile_at(i)
+        part = jnp.dot(hbuf[at, :], wbuf[2, far, :], preferred_element_type=jnp.float32)
+        q_copy(i).wait_recv()
+        racc[1, at, :] = part + rx[at, :]
+        b_copy(i).start()
 
     weigh()
 
     @pl.when(outer)
     def _():
-        mid, far, end = f + inward, f + 2 * inward, f + 3 * inward
-        for r in range(parts):
-            send_own(1, r, inward)
+        mid, away, end = f + inward, f + 2 * inward, f + 3 * inward
+        send_own(1, inward)
+        send_own(2, inward)
+        hid_copy.wait()
+        for i in range(tiles - 1):
+            h_copy(i).start()
+        send_own(3, inward)
+        h_copy(tiles - 1).start()
         gather_tokens()
-        for c in range(2):
-            add(c, block_at(f), first=True)
-        for r in range(parts):
-            take(0, mid, r)
-        add(0, block_at(mid))
+        take(0, mid)
+        add(0, near, first=True, send=True)
         score()
-        for r in range(parts):
-            take(0, far, r)
-        add(0, block_at(far))
+        take(1, mid)
+        add(1, near, first=True)
+        take(2, mid)
+        add(2, near, first=True)
+        take(3, mid)
+        add(3, near, first=True)
         reward()
-        for r in range(parts):
-            take(0, end, r)
-        add(0, block_at(end), send=True)
-        for r in range(parts):
-            take(1, mid, r)
-        add(1, block_at(mid))
+        take(1, away)
+        take(1, end)
+        add(1, far, send=True)
         advantage()
-        for r in range(parts):
-            take(1, far, r)
-        add(1, block_at(far))
-        for r in range(parts - 1):
-            take(1, end, r)
-            add(1, depth_at(end, r))
-        each(0, tiles, lambda i: x_copy(i).wait_recv())
-        take(1, end, parts - 1)
-        finish(depth_at(end, parts - 1))
+
+        def returned(i):
+            at = tile_at(i)
+            x_copy(0, i).wait_recv()
+            b_copy(i).wait_recv()
+            kv_ref[at, out_at(2)] = (acc[2, at, :] + precv[0, at, :] + rret[at, :]).astype(jnp.bfloat16)
+
+        each(0, tiles - 2, returned)
+        take(3, away)
+        add(3, block_at(away))
+        each(tiles - 2, tiles - 1, returned)
+        take(3, end)
+        finish(3, block_at(end))
+        each(tiles - 1, tiles, returned)
 
     @pl.when(inner)
     def _():
-        mine, edge, far, end = f, f + outward, f + inward, f + 2 * inward
-        send_own(1, 0, outward)
-        for r in range(parts):
-            take(0, edge, r, inward)
-        for r in range(parts):
-            send_own(1, r, inward)
-        for r in range(parts):
-            take(0, far, r, outward)
+        edge, away, end = f + outward, f + inward, f + 2 * inward
+        for q in range(1, 4):
+            send_own(q, outward)
+        take(0, edge, inward)
+        send_own(1, inward)
+        hid_copy.wait()
         gather_tokens()
-        add(0, block_at(mine), first=True)
-        for r in range(parts):
-            take(0, end, r, outward)
-        for r in range(1, parts):
-            send_own(1, r, outward)
+        take(1, edge, inward)
+        send_own(2, inward)
+        take(0, away)
+        take(0, end)
         score()
-        for r in range(parts):
-            take(1, edge, r, inward)
-        add(0, block_at(edge))
-        add(0, block_at(far))
+        add(0, whole, first=True, send=True)
+        take(2, edge, inward)
+        send_own(3, inward)
+        take(1, away, outward)
+        take(1, end, outward)
         reward()
-        add(0, block_at(end), send=True)
-        for r in range(parts):
-            take(1, far, r, outward)
-        add(1, block_at(mine), first=True)
-        add(1, block_at(edge))
-        for r in range(parts):
-            take(1, end, r, outward)
-        add(1, block_at(far))
+        spread(0)
+        add(1, whole, first=True, send=True, high=tiles // 2)
+        partial(0)
+        spread(1)
+        take(2, away)
+        partial(1)
+        add(1, whole, first=True, send=True, low=tiles // 2)
+        spread(2)
+        take(2, end)
+        give_back(0)
+        give_back(1)
+        partial(2)
+        add(2, near, first=True)
+        take(3, edge, inward)
+        take(3, away, outward)
+        give_back(2)
+        spread(3)
+        take(3, end, outward)
+        add(3, near, first=True)
+        partial(3)
+        finish(2, far)
+        give_back(3)
         advantage()
-        each(0, tiles, lambda i: x_copy(i).wait_recv())
-        finish(block_at(end))
-
-    each(0, tiles, lambda i: x_copy(i).wait_send())
+        finish(3, far)
+
+    for q in range(2):
+        each(0, tiles, lambda i: x_copy(q, i).wait_send())
     r_copy().wait_send()
     for k in range(1, n):
         v_copy(k, f).wait_send()
     each(1, plane, lambda k: s_copy(k, me).wait_send())
     each(1, n, lambda k: z_copy(k, f).wait_send())
-    for c in range(2):
+    for r in range(parts):
+        for q in range(4):
+            w_copy(q, f, r, inward).wait_send()
+
+    @pl.when(outer)
+    def _():
+        each(0, tiles, lambda i: h_copy(i).wait_send())
+
+    @pl.when(inner)
+    def _():
         for r in range(parts):
-            w_copy(c, f, r, inward).wait_send()
-
-            @pl.when(inner)
-            def _():
-                w_copy(c, f, r, outward).wait_send()
-                w_copy(c, f + outward, r, inward).wait_send()
-                w_copy(c, f + inward, r, outward).wait_send()
-                w_copy(c, f + 2 * inward, r, outward).wait_send()
+            for q in range(4):
+                w_copy(q, f, r, outward).wait_send()
+                w_copy(q, f + outward, r, inward).wait_send()
+                if q % 2:
+                    w_copy(q, f + inward, r, outward).wait_send()
+                    w_copy(q, f + 2 * inward, r, outward).wait_send()
+
+        def sent(i):
+            for k in range(3):
+                h_spread(k, i).wait_send()
+            q_copy(i).wait_send()
+            b_copy(i).wait_send()
+
+        each(0, tiles, sent)
 
 
 def solution(mesh):
@@ -567,7 +666,7 @@
         plane = nt * ns
         n_seq = lengths.shape[1]
         tile = min(256, tok)
-        in_line = n == 4 and ns == 2 and rows % 1024 == 0 and cw % 128 == 0 and tok % tile == 0
+        in_line = n == 4 and nt == 4 and ns == 2 and rows % 1024 == 0 and cw % 256 == 0 and tok % 1024 == 0
         dma = pltpu.SemaphoreType.DMA
         vmem, smem, anywhere = (
             pl.BlockSpec(memory_space=pltpu.VMEM),
@@ -577,24 +676,32 @@
         if in_line:
             body = functools.partial(line_kernel, nt, ns, parts, tile)
             tiles = tok // tile
+            qw = cw // 2
             scratch = [
                 pltpu.VMEM((tok, depth), jnp.bfloat16),
-                pltpu.VMEM((2, depth, cw), jnp.bfloat16),
-                pltpu.VMEM((2, tok, cw), jnp.float32),
-                pltpu.VMEM((tok, cw), jnp.float32),
+                pltpu.VMEM((4, depth, qw), jnp.bfloat16),
+                pltpu.VMEM((4, tok, qw), jnp.float32),
+                pltpu.VMEM((2, tok, qw), jnp.float32),
+                pltpu.VMEM((tok, 2 * rows), jnp.bfloat16),
+                pltpu.VMEM((2, tok, qw), jnp.float32),
+                pltpu.VMEM((tok, qw), jnp.float32),
+                pltpu.VMEM((tok, qw), jnp.float32),
                 pltpu.VMEM((8, tok), jnp.float32),
                 pltpu.VMEM((8, depth), jnp.float32),
                 pltpu.VMEM((1, cw), jnp.float32),
                 pltpu.VMEM((n, rows // 128, 128), jnp.float32),
                 pltpu.VMEM((plane, 8, 128), jnp.float32),
                 pltpu.VMEM((n, 2, 8, 128), jnp.float32),
-                dma, dma((2,)),
-                dma((2, 2, parts, n)), dma((2, parts, n)),
-                dma((tiles,)), dma((tiles,)),
+                dma, dma((4,)),
+                dma((2, 4, parts, n)), dma((4, parts, n)),
+                dma((2, tiles)), dma((2, tiles)),
                 dma, dma,
                 dma((n,)), dma((n,)),
                 dma((plane,)), dma((plane,)),
                 dma((n,)), dma((n,)),
+                dma((3, tiles)), dma((tiles, nt)),
+                dma((tiles,)), dma((tiles,)),
+                dma((tiles,)), dma((tiles,)),
             ]
         else:
             body = functools.partial(kernel, n, nt, ns, parts, tile)

time: 79.9 us -> 85.7 us (1.073)
  Pallas kernels: 77.8 us -> 83.6 us
    pallas_call x1, Pallas kernels: 77.8 us -> 83.6 us  [local(): pl.pallas_call(body, out_shape=(pltpu.VMEM((tok, width // 2), jnp.bfloat1...]
where the time goes in v2:
time: 85.7 us; the launch traced here: 85.5 us
  Pallas kernels  83.6 us (98%)
  local copies, waits for them, and re-layouts  1.31 us (2%)
    pallas_call x1, Pallas kernels, local(): pl.pallas_call(body, out_shape=(pltpu.VMEM((tok, width // 2), jnp.bfloat1...  83.6 us

profile of v2, /device:TPU:0, one launch (start us, length us, event | category | flops | bytes accessed | tf_op | source)
XLA Modules:
  0.0 85.5 jit_solution(8229639444486733271)
XLA Ops:
  0.6 83.6 %shard_map.77 = (bf16[1024,256]{1,0:T(8,128)(2,1)S(1)}, f32[1,4]{1,0:T(1,128)S(1)}) custom-call(bf16[1024,4096]{1,0:T(8,128)(2,1)} %hid_any.1, bf16[1024,512]{1,0:T(8,128)(2,1)} %w_any.1, f32[1,256]{1,0:T(1,128)} %bitcast.5, s32[1,1024]{1,0:T(1,128)} %bitcast.4, s32[1,4]{1,0:T(1,128)} %len_ref.1, s32[4]{0:T(128)} %gid_ref.1), custom_call_target="tpu_custom_call" | custom-call | tf_op jit(solution)/shard_map/pallas_call | solution.py:722
  84.2 0.8 copy.10
  85.0 0.5 copy.11

commit v3 on v2

--- a/solution.py
+++ b/solution.py
@@ -259,7 +259,7 @@
 
 
 def line_kernel(
-    nt, ns, parts, tile,
+    nt, ns, parts, tile, blocks,
     hid_any, w_any, ro_ref, mask_ref, len_ref, gid_ref,
     kv_ref, adv_ref,
     hid, wbuf, acc, precv, hbuf, racc, rx, rret, member, gsum, robuf, vbuf, sbuf, zbuf,
@@ -277,7 +277,8 @@
     piece = rows // parts
     tok, depth = hid.shape
     tiles = tok // tile
-    share = tile // nt
+    blk = tok // blocks
+    share = blk // nt
     inward = jnp.where(f < 2, 1, -1)
     outward = -inward
     outer = (f == 0) | (f == n - 1)
@@ -309,8 +310,11 @@
     def tile_at(i):
         return pl.ds(pl.multiple_of(i * tile, tile), tile)
 
+    def blk_at(i):
+        return pl.ds(pl.multiple_of(i * blk, blk), blk)
+
     def share_at(i, p):
-        return pl.ds(pl.multiple_of(i * tile + p * share, share), share)
+        return pl.ds(pl.multiple_of(i * blk + p * share, share), share)
 
     def remote(src, dst, send, recv, device):
         return pltpu.make_async_remote_copy(
@@ -342,11 +346,11 @@
         return remote(hbuf.at[at], hbuf.at[at], hsend.at[0, i], hrecv.at[i, p], {"tp": mate})
 
     def q_copy(i):
-        at = tile_at(i)
+        at = blk_at(i)
         return remote(racc.at[0, at], rx.at[at], qsend.at[i], qrecv.at[i], {"sect": 1 - s})
 
     def b_copy(i):
-        at = tile_at(i)
+        at = blk_at(i)
         return remote(racc.at[1, at], rret.at[at], bsend.at[i], brecv.at[i], {"fsdp": f + outward})
 
     def r_copy():
@@ -376,8 +380,8 @@
         for r in range(parts):
             w_copy(q, f, r, step, own=True).start()
 
-    def take(q, j, step=None):
-        for r in range(parts):
+    def take(q, j, step=None, low=0, high=parts):
+        for r in range(low, high):
             w_copy(q, j, r, outward).wait_recv()
             if step is not None:
                 w_copy(q, j, r, step).start()
@@ -518,22 +522,29 @@
         h_spread(0, i).start()
         h_spread(1, i).start()
 
-    def partial(i):
+    def relay(i):
         h_recv(i, across).wait_recv()
         h_spread(2, i).start()
+
+    def partial(i):
         h_recv(i, mate).wait_recv()
         h_recv(i, cross).wait_recv()
-        at = tile_at(i)
+        at = blk_at(i)
         racc[0, at, :] = jnp.dot(hbuf[at, :], wbuf[0, far, :], preferred_element_type=jnp.float32)
         q_copy(i).start()
 
     def give_back(i):
-        at = tile_at(i)
+        at = blk_at(i)
         part = jnp.dot(hbuf[at, :], wbuf[2, far, :], preferred_element_type=jnp.float32)
         q_copy(i).wait_recv()
         racc[1, at, :] = part + rx[at, :]
         b_copy(i).start()
 
+    def returned(i):
+        at = blk_at(i)
+        b_copy(i).wait_recv()
+        kv_ref[at, out_at(2)] = (acc[2, at, :] + precv[0, at, :] + rret[at, :]).astype(jnp.bfloat16)
+
     weigh()
 
     @pl.when(outer)
@@ -542,39 +553,33 @@
         send_own(1, inward)
         send_own(2, inward)
         hid_copy.wait()
-        for i in range(tiles - 1):
-            h_copy(i).start()
-        send_own(3, inward)
-        h_copy(tiles - 1).start()
+        each(0, 5, lambda i: h_copy(i).start())
+        for r in range(parts):
+            w_copy(3, f, r, inward, own=True).start()
+            h_copy(5 + r).start()
+        each(5 + parts, blocks, lambda i: h_copy(i).start())
         gather_tokens()
         take(0, mid)
         add(0, near, first=True, send=True)
         score()
-        take(1, mid)
-        add(1, near, first=True)
-        take(2, mid)
-        add(2, near, first=True)
-        take(3, mid)
-        add(3, near, first=True)
+        for q in range(1, 4):
+            take(q, mid)
+            add(q, near, first=True)
         reward()
         take(1, away)
         take(1, end)
         add(1, far, send=True)
-        advantage()
-
-        def returned(i):
-            at = tile_at(i)
-            x_copy(0, i).wait_recv()
-            b_copy(i).wait_recv()
-            kv_ref[at, out_at(2)] = (acc[2, at, :] + precv[0, at, :] + rret[at, :]).astype(jnp.bfloat16)
-
-        each(0, tiles - 2, returned)
         take(3, away)
         add(3, block_at(away))
-        each(tiles - 2, tiles - 1, returned)
-        take(3, end)
-        finish(3, block_at(end))
-        each(tiles - 1, tiles, returned)
+        each(0, tiles, lambda i: x_copy(0, i).wait_recv())
+        each(0, 6, returned)
+        advantage()
+        take(3, end, high=parts - 1)
+        for r in range(parts - 1):
+            add(3, depth_at(end, r))
+        take(3, end, low=parts - 1)
+        finish(3, depth_at(end, parts - 1))
+        each(6, blocks, returned)
 
     @pl.when(inner)
     def _():
@@ -586,40 +591,58 @@
         hid_copy.wait()
         gather_tokens()
         take(1, edge, inward)
-        send_own(2, inward)
+        send_own(3, inward)
         take(0, away)
         take(0, end)
         score()
         add(0, whole, first=True, send=True)
         take(2, edge, inward)
-        send_own(3, inward)
+        send_own(2, inward)
         take(1, away, outward)
+        add(1, near, first=True)
+        spread(0)
+        spread(1)
         take(1, end, outward)
+        relay(0)
         reward()
-        spread(0)
-        add(1, whole, first=True, send=True, high=tiles // 2)
+        add(1, far, send=True, high=tiles // 2)
+        spread(2)
         partial(0)
-        spread(1)
+        relay(1)
+        spread(3)
+        partial(1)
+        take(3, away, outward)
+        add(1, far, send=True, low=tiles // 2)
+        relay(2)
+        spread(4)
+        partial(2)
+        relay(3)
+        partial(3)
+        take(3, edge, inward, high=1)
+        add(2, near, first=True)
+        relay(4)
+        spread(5)
+        partial(4)
+        take(2, end)
         take(2, away)
-        partial(1)
-        add(1, whole, first=True, send=True, low=tiles // 2)
-        spread(2)
-        take(2, end)
-        give_back(0)
-        give_back(1)
-        partial(2)
-        add(2, near, first=True)
-        take(3, edge, inward)
-        take(3, away, outward)
-        give_back(2)
-        spread(3)
+        take(3, edge, inward, low=1)
+        each(0, 5, give_back)
+        relay(5)
+        spread(6)
+        partial(5)
+        finish(2, far)
+        spread(7)
+        give_back(5)
+        relay(6)
+        add(3, near, first=True)
         take(3, end, outward)
-        add(3, near, first=True)
-        partial(3)
-        finish(2, far)
-        give_back(3)
+        partial(6)
+        relay(7)
+        partial(7)
+        give_back(6)
+        finish(3, far)
+        give_back(7)
         advantage()
-        finish(3, far)
 
     for q in range(2):
         each(0, tiles, lambda i: x_copy(q, i).wait_send())
@@ -634,7 +657,7 @@
 
     @pl.when(outer)
     def _():
-        each(0, tiles, lambda i: h_copy(i).wait_send())
+        each(0, blocks, lambda i: h_copy(i).wait_send())
 
     @pl.when(inner)
     def _():
@@ -652,7 +675,7 @@
             q_copy(i).wait_send()
             b_copy(i).wait_send()
 
-        each(0, tiles, sent)
+        each(0, blocks, sent)
 
 
 def solution(mesh):
@@ -674,7 +697,8 @@
             pl.BlockSpec(memory_space=pl.ANY),
         )
         if in_line:
-            body = functools.partial(line_kernel, nt, ns, parts, tile)
+            blocks = 8
+            body = functools.partial(line_kernel, nt, ns, parts, tile, blocks)
             tiles = tok // tile
             qw = cw // 2
             scratch = [
@@ -699,9 +723,9 @@
                 dma((n,)), dma((n,)),
                 dma((plane,)), dma((plane,)),
                 dma((n,)), dma((n,)),
-                dma((3, tiles)), dma((tiles, nt)),
-                dma((tiles,)), dma((tiles,)),
-                dma((tiles,)), dma((tiles,)),
+                dma((3, blocks)), dma((blocks, nt)),
+                dma((blocks,)), dma((blocks,)),
+                dma((blocks,)), dma((blocks,)),
             ]
         else:
             body = functools.partial(kernel, n, nt, ns, parts, tile)

time: 85.7 us -> 74.1 us (0.86)
  Pallas kernels: 83.6 us -> 72 us
    pallas_call x1, Pallas kernels: 83.6 us -> 72 us  [local(): pl.pallas_call(body, out_shape=(pltpu.VMEM((tok, width // 2), jnp.bfloat1...]
where the time goes in v3:
time: 74.1 us; the launch traced here: 74 us
  Pallas kernels  72 us (97%)
  local copies, waits for them, and re-layouts  1.31 us (2%)
    pallas_call x1, Pallas kernels, local(): pl.pallas_call(body, out_shape=(pltpu.VMEM((tok, width // 2), jnp.bfloat1...  72 us

profile of v3, /device:TPU:0, one launch (start us, length us, event | category | flops | bytes accessed | tf_op | source)
XLA Modules:
  0.0 74.0 jit_solution(4003203730827591226)
XLA Ops:
  0.6 72.0 %shard_map.77 = (bf16[1024,256]{1,0:T(8,128)(2,1)S(1)}, f32[1,4]{1,0:T(1,128)S(1)}) custom-call(bf16[1024,4096]{1,0:T(8,128)(2,1)} %hid_any.1, bf16[1024,512]{1,0:T(8,128)(2,1)} %w_any.1, f32[1,256]{1,0:T(1,128)} %bitcast.5, s32[1,1024]{1,0:T(1,128)} %bitcast.4, s32[1,4]{1,0:T(1,128)} %len_ref.1, s32[4]{0:T(128)} %gid_ref.1), custom_call_target="tpu_custom_call" | custom-call | tf_op jit(solution)/shard_map/pallas_call | solution.py:746
  72.6 0.8 %copy.10 = bf16[1024,256]{1,0:T(8,128)(2,1)} copy(bf16[1024,256]{1,0:T(8,128)(2,1)S(1)} %get-tuple-element.6) | data formatting | bytes 1048576
  73.4 0.5 copy.11

commit v4 on v3

--- a/solution.py
+++ b/solution.py
@@ -260,8 +260,9 @@
 
 def line_kernel(
     nt, ns, parts, tile, blocks,
-    hid_any, w_any, ro_ref, mask_ref, len_ref, gid_ref,
+    hid_any, w_any, ro_any, mask_any, len_any, gid_any,
     kv_ref, adv_ref,
+    ro_ref, mask_ref, len_ref, gid_ref, small_sem,
     hid, wbuf, acc, precv, hbuf, racc, rx, rret, member, gsum, robuf, vbuf, sbuf, zbuf,
     hid_sem, own_sem, wsend, wrecv, xsend, xrecv, rsend, rrecv,
     vsend, vrecv, ssend, srecv, zsend, zrecv,
@@ -391,6 +392,13 @@
         barrier, inc=1, device_id=line_id(k), device_id_type=MESH))
     each(1, plane, lambda k: pl.semaphore_signal(
         barrier, inc=1, device_id=plane_id(k), device_id_type=MESH))
+    small = [
+        pltpu.make_async_copy(src, dst, small_sem.at[i])
+        for i, (src, dst) in enumerate((
+            (ro_any, ro_ref), (mask_any, mask_ref), (len_any, len_ref), (gid_any, gid_ref)))
+    ]
+    for copy in small:
+        copy.start()
     for q in (2, 3, 0, 1):
         own_copy(q).start()
     hid_copy = pltpu.make_async_copy(hid_any, hid, hid_sem)
@@ -403,13 +411,15 @@
     def _():
         send_own(0, outward)
 
+    for copy in small:
+        copy.wait()
     r_copy().start()
 
     place = lax.broadcasted_iota(jnp.int32, (8, tok), 1)
     seq = lax.broadcasted_iota(jnp.int32, (8, tok), 0)
     inside = jnp.zeros((8, tok), jnp.bool_)
     start = jnp.int32(0)
-    n_seq = len_ref.shape[1]
+    n_seq = len_any.shape[1]
     for j in range(n_seq):
         finish = start + len_ref[0, j]
         inside = inside | ((seq == j) & (place >= start) & (place < finish))
@@ -572,22 +582,23 @@
         take(3, away)
         add(3, block_at(away))
         each(0, tiles, lambda i: x_copy(0, i).wait_recv())
-        each(0, 6, returned)
-        advantage()
+        each(0, 5, returned)
         take(3, end, high=parts - 1)
         for r in range(parts - 1):
             add(3, depth_at(end, r))
         take(3, end, low=parts - 1)
         finish(3, depth_at(end, parts - 1))
-        each(6, blocks, returned)
+        advantage()
+        each(5, blocks, returned)
 
     @pl.when(inner)
     def _():
         edge, away, end = f + outward, f + inward, f + 2 * inward
         for q in range(1, 4):
             send_own(q, outward)
-        take(0, edge, inward)
-        send_own(1, inward)
+        for r in range(parts):
+            take(0, edge, inward, low=r, high=r + 1)
+            w_copy(1, f, r, inward, own=True).start()
         hid_copy.wait()
         gather_tokens()
         take(1, edge, inward)
@@ -601,18 +612,18 @@
         take(1, away, outward)
         add(1, near, first=True)
         spread(0)
+        take(1, end, outward)
+        reward()
         spread(1)
-        take(1, end, outward)
+        add(1, far, send=True, high=tiles // 2)
         relay(0)
-        reward()
-        add(1, far, send=True, high=tiles // 2)
         spread(2)
         partial(0)
+        spread(3)
         relay(1)
-        spread(3)
         partial(1)
         take(3, away, outward)
-        add(1, far, send=True, low=tiles // 2)
+        add(1, far, send=True, low=tiles // 2, high=tiles - 1)
         relay(2)
         spread(4)
         partial(2)
@@ -625,24 +636,26 @@
         partial(4)
         take(2, end)
         take(2, away)
+        each(0, 5, give_back)
         take(3, edge, inward, low=1)
-        each(0, 5, give_back)
         relay(5)
         spread(6)
         partial(5)
+        add(1, far, send=True, low=tiles - 1)
+        take(3, end, outward, high=1)
+        spread(7)
+        take(3, end, outward, low=1)
         finish(2, far)
-        spread(7)
+        relay(6)
+        partial(6)
         give_back(5)
-        relay(6)
-        add(3, near, first=True)
-        take(3, end, outward)
-        partial(6)
         relay(7)
         partial(7)
         give_back(6)
-        finish(3, far)
+        add(3, near, first=True)
         give_back(7)
         advantage()
+        finish(3, far)
 
     for q in range(2):
         each(0, tiles, lambda i: x_copy(q, i).wait_send())
@@ -701,7 +714,13 @@
             body = functools.partial(line_kernel, nt, ns, parts, tile, blocks)
             tiles = tok // tile
             qw = cw // 2
+            specs = [anywhere] * 6
             scratch = [
+                pltpu.VMEM((1, cw), jnp.float32),
+                pltpu.VMEM((1, tok), jnp.int32),
+                pltpu.SMEM((1, n_seq), jnp.int32),
+                pltpu.SMEM((n_seq,), jnp.int32),
+                dma((4,)),
                 pltpu.VMEM((tok, depth), jnp.bfloat16),
                 pltpu.VMEM((4, depth, qw), jnp.bfloat16),
                 pltpu.VMEM((4, tok, qw), jnp.float32),
@@ -729,6 +748,7 @@
             ]
         else:
             body = functools.partial(kernel, n, nt, ns, parts, tile)
+            specs = [anywhere, anywhere, vmem, vmem, smem, smem]
             scratch = [
                 pltpu.VMEM((tok, depth), jnp.bfloat16),
                 pltpu.VMEM((2, depth, cw), jnp.bfloat16),
@@ -749,7 +769,7 @@
                 pltpu.VMEM((tok, width // 2), jnp.bfloat16),
                 pltpu.VMEM((1, n_seq), jnp.float32),
             ),
-            in_specs=[anywhere, anywhere, vmem, vmem, smem, smem],
+            in_specs=specs,
             out_specs=(vmem, vmem),
             scratch_shapes=scratch,
             compiler_params=pltpu.CompilerParams(collective_id=0, has_side_effects=True),

time: 74.1 us -> 70.9 us (0.957)
  Pallas kernels: 72 us -> 68.8 us
    pallas_call x1, Pallas kernels: 72 us -> 68.8 us  [local(): pl.pallas_call(body, out_shape=(pltpu.VMEM((tok, width // 2), jnp.bfloat1...]
where the time goes in v4:
time: 70.9 us; the launch traced here: 70.8 us
  Pallas kernels  68.8 us (97%)
  local copies, waits for them, and re-layouts  1.31 us (2%)
    pallas_call x1, Pallas kernels, local(): pl.pallas_call(body, out_shape=(pltpu.VMEM((tok, width // 2), jnp.bfloat1...  68.8 us

profile of v4, /device:TPU:0, one launch (start us, length us, event | category | flops | bytes accessed | tf_op | source)
XLA Modules:
  0.0 70.8 jit_solution(4306649216518621534)
XLA Ops:
  0.6 68.8 %shard_map.77 = (bf16[1024,256]{1,0:T(8,128)(2,1)S(1)}, f32[1,4]{1,0:T(1,128)S(1)}) custom-call(bf16[1024,4096]{1,0:T(8,128)(2,1)} %hid_any.1, bf16[1024,512]{1,0:T(8,128)(2,1)} %w_any.1, f32[1,256]{1,0:T(1,128)} %bitcast.5, s32[1,1024]{1,0:T(1,128)} %bitcast.4, s32[1,4]{1,0:T(1,128)} %len_any.1, s32[4]{0:T(128)} %gid_any.1), custom_call_target="tpu_custom_call" | custom-call | tf_op jit(solution)/shard_map/pallas_call | solution.py:766
  69.5 0.8 %copy.10 = bf16[1024,256]{1,0:T(8,128)(2,1)} copy(bf16[1024,256]{1,0:T(8,128)(2,1)S(1)} %get-tuple-element.6) | data formatting | bytes 1048576
  70.3 0.5 copy.11

commit v5 on v4

--- a/solution.py
+++ b/solution.py
@@ -266,7 +266,7 @@
     hid, wbuf, acc, precv, hbuf, racc, rx, rret, member, gsum, robuf, vbuf, sbuf, zbuf,
     hid_sem, own_sem, wsend, wrecv, xsend, xrecv, rsend, rrecv,
     vsend, vrecv, ssend, srecv, zsend, zrecv,
-    hsend, hrecv, qsend, qrecv, bsend, brecv,
+    hsend, hrecv, qsend, qrecv, bsend, brecv, line_in, plane_in,
 ):
     n = 4
     f, t, s = lax.axis_index("fsdp"), lax.axis_index("tp"), lax.axis_index("sect")
@@ -387,11 +387,19 @@
             if step is not None:
                 w_copy(q, j, r, step).start()
 
+    def tell(semaphore, device):
+        pl.semaphore_signal(semaphore, inc=1, device_id=device, device_id_type=MESH)
+
     barrier = pltpu.get_barrier_semaphore()
-    each(1, n, lambda k: pl.semaphore_signal(
-        barrier, inc=1, device_id=line_id(k), device_id_type=MESH))
-    each(1, plane, lambda k: pl.semaphore_signal(
-        barrier, inc=1, device_id=plane_id(k), device_id_type=MESH))
+    beside = ({"sect": 1 - s}, {"tp": across}, {"tp": mate})
+    tell(barrier, {"fsdp": f + inward})
+
+    @pl.when(inner)
+    def _():
+        tell(barrier, {"fsdp": f + outward})
+
+    for device in beside:
+        tell(barrier, device)
     small = [
         pltpu.make_async_copy(src, dst, small_sem.at[i])
         for i, (src, dst) in enumerate((
@@ -403,14 +411,18 @@
         own_copy(q).start()
     hid_copy = pltpu.make_async_copy(hid_any, hid, hid_sem)
     hid_copy.start()
-    pl.semaphore_wait(barrier, n - 1 + plane - 1)
+    pl.semaphore_wait(barrier, jnp.where(outer, 4, 5))
 
     send_own(0, inward)
 
     @pl.when(inner)
     def _():
         send_own(0, outward)
-
+        tell(line_in.at[0], {"fsdp": f + inward})
+        tell(line_in.at[0], {"fsdp": f + outward})
+
+    for device in beside:
+        tell(plane_in.at[0], device)
     for copy in small:
         copy.wait()
     r_copy().start()
@@ -446,6 +458,18 @@
         total = jnp.sum(total, axis=0, keepdims=True)
         for i in range(rows // 128):
             vbuf[f, i:i + 1, :] = total[:, i * 128:(i + 1) * 128]
+        pl.semaphore_wait(plane_in.at[0], 3)
+        tell(plane_in.at[1], {"sect": 1 - s})
+        pl.semaphore_wait(line_in.at[0], 1)
+
+        @pl.when(inner)
+        def _():
+            tell(line_in.at[1], {"fsdp": f + outward})
+
+        @pl.when(outer)
+        def _():
+            pl.semaphore_wait(line_in.at[1], 1)
+
         for k in range(1, n):
             v_copy(k, f).start()
 
@@ -468,6 +492,7 @@
                 at = j * rows + i * 128
                 total += gsum[:, at:at + 128] * vbuf[j, i:i + 1, :]
         sbuf[me] = jnp.broadcast_to(jnp.sum(total, axis=1, keepdims=True), (8, 128))
+        pl.semaphore_wait(plane_in.at[1], 1)
         each(1, plane, lambda k: s_copy(k, me).start())
 
     row = lax.broadcasted_iota(jnp.int32, (8, 128), 0)
@@ -745,6 +770,7 @@
                 dma((3, blocks)), dma((blocks, nt)),
                 dma((blocks,)), dma((blocks,)),
                 dma((blocks,)), dma((blocks,)),
+                pltpu.SemaphoreType.REGULAR((2,)), pltpu.SemaphoreType.REGULAR((2,)),
             ]
         else:
             body = functools.partial(kernel, n, nt, ns, parts, tile)

time: 70.9 us -> 69.4 us (0.979)
  Pallas kernels: 68.8 us -> 67.3 us
    pallas_call x1, Pallas kernels: 68.8 us -> 67.3 us  [local(): pl.pallas_call(body, out_shape=(pltpu.VMEM((tok, width // 2), jnp.bfloat1...]
where the time goes in v5:
time: 69.4 us; the launch traced here: 69.2 us
  Pallas kernels  67.3 us (97%)
  local copies, waits for them, and re-layouts  1.31 us (2%)
    pallas_call x1, Pallas kernels, local(): pl.pallas_call(body, out_shape=(pltpu.VMEM((tok, width // 2), jnp.bfloat1...  67.3 us

profile of v5, /device:TPU:0, one launch (start us, length us, event | category | flops | bytes accessed | tf_op | source)
XLA Modules:
  0.0 69.2 jit_solution(16347243725076448177)
XLA Ops:
  0.6 67.3 %shard_map.77 = (bf16[1024,256]{1,0:T(8,128)(2,1)S(1)}, f32[1,4]{1,0:T(1,128)S(1)}) custom-call(bf16[1024,4096]{1,0:T(8,128)(2,1)} %hid_any.1, bf16[1024,512]{1,0:T(8,128)(2,1)} %w_any.1, f32[1,256]{1,0:T(1,128)} %bitcast.5, s32[1,1024]{1,0:T(1,128)} %bitcast.4, s32[1,4]{1,0:T(1,128)} %len_any.1, s32[4]{0:T(128)} %gid_any.1), custom_call_target="tpu_custom_call" | custom-call | tf_op jit(solution)/shard_map/pallas_call | solution.py:792
  67.9 0.8 %copy.10 = bf16[1024,256]{1,0:T(8,128)(2,1)} copy(bf16[1024,256]{1,0:T(8,128)(2,1)S(1)} %get-tuple-element.6) | data formatting | bytes 1048576
  68.7 0.5 copy.11

commit v6 on v5

--- a/solution.py
+++ b/solution.py
@@ -580,12 +580,19 @@
         b_copy(i).wait_recv()
         kv_ref[at, out_at(2)] = (acc[2, at, :] + precv[0, at, :] + rret[at, :]).astype(jnp.bfloat16)
 
+    @pl.when(outer)
+    def _():
+        send_own(1, inward)
+
+    @pl.when(inner)
+    def _():
+        send_own(1, outward)
+
     weigh()
 
     @pl.when(outer)
     def _():
         mid, away, end = f + inward, f + 2 * inward, f + 3 * inward
-        send_own(1, inward)
         send_own(2, inward)
         hid_copy.wait()
         each(0, 5, lambda i: h_copy(i).start())
@@ -619,7 +626,7 @@
     @pl.when(inner)
     def _():
         edge, away, end = f + outward, f + inward, f + 2 * inward
-        for q in range(1, 4):
+        for q in range(2, 4):
             send_own(q, outward)
         for r in range(parts):
             take(0, edge, inward, low=r, high=r + 1)
@@ -669,11 +676,11 @@
         add(1, far, send=True, low=tiles - 1)
         take(3, end, outward, high=1)
         spread(7)
+        finish(2, far)
         take(3, end, outward, low=1)
-        finish(2, far)
         relay(6)
+        give_back(5)
         partial(6)
-        give_back(5)
         relay(7)
         partial(7)
         give_back(6)

time: 69.4 us -> 69.3 us (level)
  no operation moved by 1% of the time
where the time goes in v6:
time: 69.3 us; the launch traced here: 69.2 us
  Pallas kernels  67.2 us (97%)
  local copies, waits for them, and re-layouts  1.31 us (2%)
    pallas_call x1, Pallas kernels, local(): pl.pallas_call(body, out_shape=(pltpu.VMEM((tok, width // 2), jnp.bfloat1...  67.2 us

profile of v6, /device:TPU:0, one launch (start us, length us, event | category | flops | bytes accessed | tf_op | source)
XLA Modules:
  0.0 69.2 jit_solution(5921775962662701533)
XLA Ops:
  0.6 67.2 %shard_map.77 = (bf16[1024,256]{1,0:T(8,128)(2,1)S(1)}, f32[1,4]{1,0:T(1,128)S(1)}) custom-call(bf16[1024,4096]{1,0:T(8,128)(2,1)} %hid_any.1, bf16[1024,512]{1,0:T(8,128)(2,1)} %w_any.1, f32[1,256]{1,0:T(1,128)} %bitcast.5, s32[1,1024]{1,0:T(1,128)} %bitcast.4, s32[1,4]{1,0:T(1,128)} %len_any.1, s32[4]{0:T(128)} %gid_any.1), custom_call_target="tpu_custom_call" | custom-call | tf_op jit(solution)/shard_map/pallas_call | solution.py:799
  67.9 0.8 %copy.10 = bf16[1024,256]{1,0:T(8,128)(2,1)} copy(bf16[1024,256]{1,0:T(8,128)(2,1)S(1)} %get-tuple-element.6) | data formatting | bytes 1048576
  68.7 0.5 copy.11
